TPU v7x, 128 devices: a whole 4x4x4 slice. The times are simulated.
128 devices in a mesh: rep: 32 (over z, x, core), tp: 4 (over y).
Axes of the slice: x: 4, y: 4, z: 4, core: 2. Of those that a mesh axis runs over, the one named last changes fastest.
Arguments:
- hidden_in: bfloat16 [4096, 2048], P('rep'), may hold values from -6 to 6
- new_lengths: int32 [32, 4], P('rep'), may hold values from 1 to 64, 128 in all within a row
- prefix_lengths: int32 [32, 4], P('rep'), may hold values from 1 to 512, 1024 in all within a row
- cache_keys: bfloat16 [32768, 2048], P('rep', 'tp'), may hold values from -6 to 6
- cache_values: bfloat16 [32768, 2048], P('rep', 'tp'), may hold values from -6 to 6
- attn_gain: float32 [2048], replicated, may hold values from 0.1 to 1.9
- w_qkv: bfloat16 [2048, 3, 2048], P(None, None, 'tp'), may hold values from -1 to 1
- norm_gains: float32 [2, 2048], P(None, 'tp'), may hold values from 0 to 11
- w_out: bfloat16 [2048, 2048], P('tp'), may hold values from -0.125 to 0.125
- moe_gain: float32 [2048], replicated, may hold values from 0.1 to 1.9
- expert_ids: int32 [4096, 8], P('rep'), may hold values from 0 to 63, all different within a row; in each aligned block of 32 rows (0 to 31, 32 to 63, ...) at most 6 rows name the same one
- expert_weights: float32 [4096, 8], P('rep'), may hold values from 0.05 to 0.5
- w_gate_up: bfloat16 [64, 2048, 2, 1024], P('rep', None, None, 'tp'), may hold values from -0.125 to 0.125
- w_down: bfloat16 [64, 1024, 2048], P('rep', 'tp'), may hold values from -0.1875 to 0.1875
- next_gain: float32 [2048], replicated, may hold values from 0.1 to 1.9
- next_qkv: bfloat16 [2048, 3, 2048], P(None, None, 'tp'), may hold values from -1 to 1
- next_norm_gains: float32 [2, 2048], P(None, 'tp'), may hold values from 0.1 to 1.9
Outputs:
- hidden_out: bfloat16 [4096, 2048], P('rep')
- next_qkv_out: bfloat16 [4096, 3, 2048], P('rep', None, 'tp')
Inputs may be any that keep to these rules, and one draw needn't show every extreme that they name: `expert_ids`: in every aligned block of 32 tokens no expert is chosen more than 6 times, and some block reaches 6; a token's 8 experts differ. `new_lengths`: each replica's lengths sum to 128; its longest request has exactly 64 new tokens. `prefix_lengths`: each replica's prefix lengths sum to 1024; its longest prefix has exactly 512 tokens.
All inputs are finite; a program needn't handle non-finite values.
Results may differ from a plain program's by a relative error of at most 0.023.
Values may be sent and summed in bfloat16 or wider, within the bound.
A program may use at most 128 MiB of HBM per device.

v0:
```python
import math
import jax
import jax.numpy as jnp
from jax import lax
from jax.sharding import PartitionSpec as P

HD = 128
eps_norm = 1e-05
eps_head = 1e-06
rope_base = 10000.0


def rms_scale(inputs, gain):
    inputs = inputs.astype(jnp.float32)
    scaled = inputs * lax.rsqrt(jnp.mean(inputs * inputs, axis=-1, keepdims=True) + eps_norm)
    return (scaled * gain).astype(jnp.bfloat16)


def request_tables(new_lengths, prefix_lengths, row_count, cache_count):
    new_end = jnp.cumsum(new_lengths, dtype=jnp.int32)
    cache_end = jnp.cumsum(prefix_lengths, dtype=jnp.int32)
    token_index = jnp.arange(row_count, dtype=jnp.int32)
    cache_index = jnp.arange(cache_count, dtype=jnp.int32)
    token_request = jnp.sum(
        (token_index[:, None] >= new_end[None, :]).astype(jnp.int32), axis=1, dtype=jnp.int32
    )
    cache_request = jnp.sum(
        (cache_index[:, None] >= cache_end[None, :]).astype(jnp.int32), axis=1, dtype=jnp.int32
    )
    requests = new_lengths.shape[0]
    selector = token_request[:, None] == jnp.arange(requests, dtype=jnp.int32)[None, :]
    new_start = new_end - new_lengths
    offset = token_index - jnp.sum(
        jnp.where(selector, new_start[None, :], 0), axis=1, dtype=jnp.int32
    )
    position = offset + jnp.sum(
        jnp.where(selector, prefix_lengths[None, :], 0), axis=1, dtype=jnp.int32
    )
    return (token_request, cache_request, position)


def project_heads(normed, weight, gains, position, head_size):
    row_count = normed.shape[0]
    proj_width = weight.shape[2]
    full_width = proj_width * lax.axis_size("tp")
    projected = jnp.dot(
        normed, weight.reshape(weight.shape[0], 3 * proj_width), preferred_element_type=jnp.float32
    )
    projected = projected.reshape(row_count, 3, proj_width)
    squares = jnp.sum(projected[:, :2, :] * projected[:, :2, :], axis=2)
    totals = lax.psum(squares, "tp")
    inverse = lax.rsqrt(totals / full_width + eps_head)
    head_count = proj_width // head_size
    half_size = head_size // 2
    frequency = rope_base ** (-jnp.arange(half_size, dtype=jnp.float32) * 2.0 / head_size)
    angles = position.astype(jnp.float32)[:, None] * frequency[None, :]
    cosine = jnp.cos(angles)[:, None, :]
    sine_table = jnp.sin(angles)[:, None, :]
    outputs = []
    for member in range(2):
        member_rows = projected[:, member, :] * inverse[:, member : member + 1]
        portion = (member_rows * gains[member][None, :]).reshape(row_count, head_count, head_size)
        lower_half = portion[..., :half_size]
        upper_half = portion[..., half_size:]
        turned = jnp.concatenate(
            [
                lower_half * cosine - upper_half * sine_table,
                upper_half * cosine + lower_half * sine_table,
            ],
            axis=-1,
        )
        outputs.append(turned.reshape(row_count, proj_width).astype(jnp.bfloat16))
    outputs.append(projected[:, 2, :].astype(jnp.bfloat16))
    return jnp.stack(outputs, axis=1)


def attend(qkv, key_cache, value_cache, token_request, cache_request, head_size):
    row_count = qkv.shape[0]
    proj_width = qkv.shape[2]
    head_count = proj_width // head_size
    queries = qkv[:, 0, :].reshape(row_count, head_count, head_size)
    key_rows = jnp.concatenate([key_cache, qkv[:, 1, :]], axis=0).reshape(-1, head_count, head_size)
    value_rows = jnp.concatenate([value_cache, qkv[:, 2, :]], axis=0).reshape(
        -1, head_count, head_size
    )
    scores = jnp.einsum(
        "qhd,khd->hqk", queries, key_rows, preferred_element_type=jnp.float32
    ) / math.sqrt(head_size)
    token_index = jnp.arange(row_count, dtype=jnp.int32)
    cache_ok = cache_request[None, :] == token_request[:, None]
    new_ok = (token_request[None, :] == token_request[:, None]) & (
        token_index[None, :] <= token_index[:, None]
    )
    allowed = jnp.concatenate([cache_ok, new_ok], axis=1)
    scores = jnp.where(allowed[None], scores, -1e30)
    row_max = jnp.max(scores, axis=-1, keepdims=True)
    weights = jnp.exp(scores - row_max)
    weights = (weights / jnp.sum(weights, axis=-1, keepdims=True)).astype(jnp.bfloat16)
    context = jnp.einsum("hqk,khd->qhd", weights, value_rows, preferred_element_type=jnp.float32)
    return context.reshape(row_count, proj_width).astype(jnp.bfloat16)


def slot_ranks(expert_rows, expert_count):
    onehot = (
        expert_rows[:, :, None] == jnp.arange(expert_count, dtype=jnp.int32)[None, None, :]
    ).astype(jnp.int32)
    before = jnp.cumsum(onehot, axis=1, dtype=jnp.int32) - onehot
    return jnp.sum(before * onehot, axis=2, dtype=jnp.int32)


def expert_rows(received, w_gate_up, w_down):
    sources, local_count, slot_count, model_width = received.shape
    hidden_size = w_gate_up.shape[3]
    results = []
    for expert_slot in range(local_count):
        gathered = received[:, expert_slot].reshape(sources * slot_count, model_width)
        gate_up_out = jnp.dot(
            gathered,
            w_gate_up[expert_slot].reshape(model_width, 2 * hidden_size),
            preferred_element_type=jnp.float32,
        )
        activated = (
            jax.nn.silu(gate_up_out[:, :hidden_size]) * gate_up_out[:, hidden_size:]
        ).astype(jnp.bfloat16)
        portion = jnp.dot(
            activated, w_down[expert_slot], preferred_element_type=jnp.float32
        ).astype(jnp.bfloat16)
        results.append(portion.reshape(sources, slot_count, model_width))
    return jnp.stack(results, axis=1)


def per_device(
    hidden_in,
    new_lengths,
    prefix_lengths,
    cache_keys,
    cache_values,
    attn_gain,
    w_qkv,
    norm_gains,
    w_out,
    moe_gain,
    expert_ids,
    expert_weights,
    w_gate_up,
    w_down,
    next_gain,
    next_qkv,
    next_norm_gains,
):
    row_count, model_width = hidden_in.shape
    cache_count = cache_keys.shape[0]
    tp_count = lax.axis_size("tp")
    rep_count = lax.axis_size("rep")
    choose_count = expert_ids.shape[1]
    local_count = w_gate_up.shape[0]
    expert_count = local_count * rep_count
    quarter = row_count // tp_count
    slot_cap = max(2, quarter * choose_count * 3 // (2 * expert_count))
    full_cap = tp_count * slot_cap
    token_request, cache_request, position = request_tables(
        new_lengths[0], prefix_lengths[0], row_count, cache_count
    )
    normed = rms_scale(hidden_in, attn_gain)
    qkv = project_heads(normed, w_qkv, norm_gains, position, HD)
    context = attend(qkv, cache_keys, cache_values, token_request, cache_request, HD)
    attn_part = jnp.dot(context, w_out, preferred_element_type=jnp.float32)
    attn_out = lax.psum(attn_part.astype(jnp.bfloat16), "tp").astype(jnp.float32)
    mid_stream = (hidden_in.astype(jnp.float32) + attn_out).astype(jnp.bfloat16)
    moe_input = rms_scale(mid_stream, moe_gain)
    rank_of = slot_ranks(
        expert_ids.reshape(tp_count, quarter * choose_count), expert_count
    ).reshape(-1)
    ids_flat = expert_ids.reshape(-1)
    entry = jnp.arange(row_count * choose_count, dtype=jnp.int32)
    quarter_of = entry // (quarter * choose_count)
    flat_slot = ids_flat * full_cap + quarter_of * slot_cap + rank_of
    slot_table = (
        jnp.full((expert_count * full_cap,), row_count, jnp.int32)
        .at[flat_slot]
        .set(entry // choose_count)
    )
    padded = jnp.concatenate([moe_input, jnp.zeros((1, model_width), jnp.bfloat16)], axis=0)
    outgoing = padded[slot_table].reshape(rep_count, local_count, full_cap, model_width)
    produced = expert_rows(
        lax.all_to_all(outgoing, "rep", split_axis=0, concat_axis=0, tiled=True), w_gate_up, w_down
    )
    returned = lax.all_to_all(produced, "rep", split_axis=0, concat_axis=0, tiled=True)
    picked = returned.reshape(expert_count * full_cap, model_width)[flat_slot].astype(jnp.float32)
    partial_value = jnp.sum(
        picked.reshape(row_count, choose_count, model_width) * expert_weights[:, :, None], axis=1
    )
    moe_out = lax.psum(partial_value.astype(jnp.bfloat16), "tp").astype(jnp.float32)
    hidden_out = (mid_stream.astype(jnp.float32) + moe_out).astype(jnp.bfloat16)
    next_input = rms_scale(hidden_out, next_gain)
    next_qkv_out = project_heads(next_input, next_qkv, next_norm_gains, position, HD)
    return (hidden_out, next_qkv_out)


def solution(mesh):
    placed = (
        P("rep", None),
        P("rep", None),
        P("rep", None),
        P("rep", "tp"),
        P("rep", "tp"),
        P(),
        P(None, None, "tp"),
        P(None, "tp"),
        P("tp", None),
        P(),
        P("rep", None),
        P("rep", None),
        P("rep", None, None, "tp"),
        P("rep", "tp", None),
        P(),
        P(None, None, "tp"),
        P(None, "tp"),
    )
    return jax.shard_map(
        per_device,
        mesh=mesh,
        in_specs=placed,
        out_specs=(P("rep", None), P("rep", None, "tp")),
        check_vma=False,
    )
```

profile of v0, /device:TPU:0, one launch (start us, length us, event | category | flops | bytes accessed | tf_op | source)
XLA Modules:
  0.0 372.7 jit_solution(4477578113990545724)
XLA Ops:
  7.2 9.0 %copy.73 = bf16[2048,3,512]{0,2,1:T(8,128)(2,1)} copy(bf16[2048,3,512]{2,0,1:T(8,128)(2,1)} %param.23) | data formatting | bytes 12582912 | tf_op args[6]
  16.4 5.0 %fusion.4 = f32[128,3,512]{2,0,1:T(8,128)S(1)} fusion(bf16[2048,3,512]{0,2,1:T(8,128)(2,1)} %copy.73, bf16[128,2048]{1,0:T(8,128)(2,1)S(1)} %copy-done.2, f32[2048]{0:T(1024)S(1)} %copy-done.9, f32[128]{0:T(128)S(1)} %add_rsqrt_fusion.4), kind=kOutput, calls=%fused_computation.9 | convolution fusion | flops 806354944 | bytes 7610880 | tf_op jit(solution)/shard_map/dot_general | solution.py:46
  22.4 10.8 %psum.28 = f32[128,2]{0,1:T(2,128)S(1)} all-reduce(f32[128,2]{0,1:T(2,128)S(1)} %fusion.33), channel_id=1, replica_groups=mesh['rep'=32,'tp'=4] {'tp'}, use_global_device_ids=true, to_apply=%region_6.7 | all-reduce | flops 256 | bytes 2048 | tf_op jit(solution)/shard_map/psum | solution.py:51
  41.6 2.4 copy.74
  44.1 2.3 pad_maximum_fusion.2
  46.4 3.7 fusion.83
  50.1 2.6 fusion.10
  54.4 2.4 reduce-window.25
  57.5 4.3 %scatter_custom_fusion = s32[1536]{0:T(1024)S(1)} fusion(s32[1024]{0:T(1024)S(1)} %bitcast.137, s32[1024]{0:T(1024)S(1)} %add_select_fusion, s32[]{:T(128)} %constant.74.clone.1), kind=kCustom, calls=%fused_computation.120 | custom fusion | bytes 6148 | tf_op jit(solution)/shard_map/scatter | solution.py:181
  61.8 35.4 %all-reduce.4.cloned.1.call-done = bf16[128,2048]{1,0:T(8,128)(2,1)} async-done(((bf16[128,2048]{1,0:T(8,128)(2,1)}), bf16[128,2048]{1,0:T(8,128)(2,1)}) %all-reduce.4.cloned.1.call-update) | async-done | bytes 524304 | tf_op jit(solution)/shard_map/psum | solution.py:168
  99.8 7.1 %gather_fusion = bf16[1536,2048]{1,0:T(8,128)(2,1)} fusion(bf16[129,2048]{1,0:T(8,128)(2,1)S(1)} %concatenate.33, s32[2048]{0:T(1024)S(1)} %pad_clamp_fusion), kind=kCustom, calls=%fused_computation | custom fusion | bytes 12589056 | tf_op jit(solution)/shard_map/gather | solution.py:184
  106.9 7.5 %all-to-all-start = ((bf16[32,2,24,2048]{3,2,1,0:T(8,128)(2,1)}), bf16[32,2,24,2048]{3,2,1,0:T(8,128)(2,1)}, u32[]{:S(2)}, u32[]{:S(2)}) async-start(bf16[32,2,24,2048]{3,2,1,0:T(8,128)(2,1)} %bitcast.119), calls=%async_computation | async-start | bytes 12582912 | tf_op jit(solution)/shard_map/all_to_all | solution.py:186
  114.5 4.7 %fusion.78 = (bf16[1,2048,2,256]{3,2,1,0:T(2,128)(2,1)S(1)}, bf16[1,2048,2,256]{3,2,1,0:T(2,128)(2,1)S(1)}) fusion(bf16[2,2048,2,256]{3,2,1,0:T(2,128)(2,1)} %param.29), kind=kLoop, calls=%fused_computation.151 | loop fusion | bytes 8388608 | tf_op jit(solution)/shard_map/slice | solution.py:119
  122.8 69.3 %all-to-all-done = bf16[32,2,24,2048]{3,2,1,0:T(8,128)(2,1)} async-done(((bf16[32,2,24,2048]{3,2,1,0:T(8,128)(2,1)}), bf16[32,2,24,2048]{3,2,1,0:T(8,128)(2,1)}, u32[]{:S(2)}, u32[]{:S(2)}) %all-to-all-start) | async-done | bytes 6291488 | tf_op jit(solution)/shard_map/all_to_all | solution.py:186
  192.2 3.4 fusion.77
  201.8 3.2 pad_maximum_fusion
  205.1 5.0 %all-to-all-start.1 = ((bf16[32,2,24,2048]{3,2,1,0:T(8,128)(2,1)}), bf16[32,2,24,2048]{3,2,1,0:T(8,128)(2,1)}, u32[]{:S(2)}, u32[]{:S(2)}) async-start(bf16[32,2,24,2048]{3,2,1,0:T(8,128)(2,1)} %pad_maximum_fusion), calls=%async_computation.1 | async-start | bytes 12582912 | tf_op jit(solution)/shard_map/all_to_all | solution.py:188
  210.5 77.5 %all-to-all-done.1 = bf16[32,2,24,2048]{3,2,1,0:T(8,128)(2,1)} async-done(((bf16[32,2,24,2048]{3,2,1,0:T(8,128)(2,1)}), bf16[32,2,24,2048]{3,2,1,0:T(8,128)(2,1)}, u32[]{:S(2)}, u32[]{:S(2)}) %all-to-all-start.1) | async-done | bytes 6291488 | tf_op jit(solution)/shard_map/all_to_all | solution.py:188
  288.0 12.4 %gather_fusion.1 = bf16[1024,2048]{1,0:T(8,128)(2,1)} fusion(bf16[1536,2048]{1,0:T(8,128)(2,1)} %bitcast.33, s32[1024]{0:T(1024)S(1)} %broadcast_clamp_fusion), kind=kCustom, calls=%fused_computation.1 | custom fusion | bytes 8392704 | tf_op jit(solution)/shard_map/gather | solution.py:189
  300.4 7.3 %fusion.1 = bf16[128,2048]{1,0:T(8,128)(2,1)} fusion(bf16[1024,2048]{1,0:T(8,128)(2,1)} %gather_fusion.1, f32[128,8]{1,0:T(8,128)S(1)} %copy.88), kind=kLoop, calls=%fused_computation.5 | loop fusion | flops 6029312 | bytes 4722688 | tf_op jit(solution)/shard_map/reduce_sum | solution.py:190
  307.8 8.9 %copy.89 = bf16[2048,3,512]{0,2,1:T(8,128)(2,1)} copy(bf16[2048,3,512]{2,0,1:T(8,128)(2,1)} %param.32) | data formatting | bytes 12582912 | tf_op args[15]
  316.7 30.3 %all-reduce.6.cloned.1.call-done = bf16[128,2048]{1,0:T(8,128)(2,1)} async-done(((bf16[128,2048]{1,0:T(8,128)(2,1)}), bf16[128,2048]{1,0:T(8,128)(2,1)}) %all-reduce.6.cloned.1.call-update) | async-done | bytes 524304 | tf_op jit(solution)/shard_map/psum | solution.py:193
  348.4 5.2 %fusion.2 = f32[128,3,512]{2,0,1:T(8,128)S(1)} fusion(bf16[2048,3,512]{0,2,1:T(8,128)(2,1)} %copy.89, bf16[128,2048]{1,0:T(8,128)(2,1)S(1)} %get-tuple-element.5, f32[2048]{0:T(1024)S(1)} %copy-done.11, f32[128]{0:T(128)S(1)} %add_rsqrt_fusion.2), kind=kOutput, calls=%fused_computation.7 | convolution fusion | flops 806354944 | bytes 7610880 | tf_op jit(solution)/shard_map/dot_general | solution.py:46
  354.1 9.5 %psum.31 = f32[128,2]{0,1:T(2,128)S(1)} all-reduce(f32[128,2]{0,1:T(2,128)S(1)} %fusion.32), channel_id=1, replica_groups=mesh['rep'=32,'tp'=4] {'tp'}, use_global_device_ids=true, to_apply=%region_21.22 | all-reduce | flops 256 | bytes 2048 | tf_op jit(solution)/shard_map/psum | solution.py:51
  (125 shorter events, 28.7 us)
Async XLA Ops:
  7.2 45.6 %copy-start = (bf16[512,2048]{1,0:T(8,128)(2,1)S(1)}, bf16[512,2048]{1,0:T(8,128)(2,1)}, u32[]{:S(2)}) copy-start(bf16[512,2048]{1,0:T(8,128)(2,1)} %param.25) | copy-start | bytes 6291460
  7.2 9.1 %copy-start.2 = (bf16[128,2048]{1,0:T(8,128)(2,1)S(1)}, bf16[128,2048]{1,0:T(8,128)(2,1)}, u32[]{:S(2)}) copy-start(bf16[128,2048]{1,0:T(8,128)(2,1)} %param.17) | copy-start | bytes 1572868
  7.2 9.3 %copy-start.9 = (f32[2048]{0:T(1024)S(1)}, f32[2048]{0:T(1024)}, u32[]{:S(2)}) copy-start(f32[2048]{0:T(1024)} %param.22) | copy-start | bytes 24580
  7.2 90.0 %all-reduce.4.cloned.1.call-start = ((), (), s32[]{:S(2)}) async-start(), calls=%async_computation.2 | async-start | bytes 1048576 | tf_op jit(solution)/shard_map/psum | solution.py:168
  21.5 11.8 %copy-start.15 = (f32[2,512]{1,0:T(2,128)S(1)}, f32[2,512]{1,0:T(2,128)}, u32[]{:S(2)}) copy-start(f32[2,512]{1,0:T(2,128)} %param.24) | copy-start | bytes 12292
  21.5 11.8 %copy-start.19 = (s32[1,4]{1,0:T(1,128)S(1)}, s32[1,4]{1,0:T(1,128)}, u32[]{:S(2)}) copy-start(s32[1,4]{1,0:T(1,128)} %param.18) | copy-start | bytes 52
  33.5 1.9 copy-start.12
  35.5 3.4 copy-start.17
  35.5 3.7 copy-start.13
  41.6 4.7 %copy-start.7 = (bf16[128,4,64]{2,0,1:T(8,128)(2,1)S(1)}, bf16[128,4,64]{2,0,1:T(8,128)(2,1)}, u32[]{:S(2)}) copy-start(bf16[128,4,64]{2,0,1:T(8,128)(2,1)} %get-tuple-element.19) | copy-start | bytes 196612
  52.7 1.3 copy-start.8
  54.0 44.5 %copy-start.10 = (f32[2048]{0:T(1024)S(1)}, f32[2048]{0:T(1024)}, u32[]{:S(2)}) copy-start(f32[2048]{0:T(1024)} %param.26) | copy-start | bytes 24580
  106.9 85.2 %all-to-all-start = ((bf16[32,2,24,2048]{3,2,1,0:T(8,128)(2,1)}), bf16[32,2,24,2048]{3,2,1,0:T(8,128)(2,1)}, u32[]{:S(2)}, u32[]{:S(2)}) async-start(bf16[32,2,24,2048]{3,2,1,0:T(8,128)(2,1)} %bitcast.119), calls=%async_computation | async-start | bytes 12582912 | tf_op jit(solution)/shard_map/all_to_all | solution.py:186
  122.8 72.8 %copy-start.6 = (bf16[256,8,2,256]{3,1,2,0:T(8,128)(2,1)S(1)}, bf16[256,8,2,256]{3,1,2,0:T(8,128)(2,1)}, u32[]{:S(2)}) copy-start(bf16[256,8,2,256]{3,1,2,0:T(8,128)(2,1)} %copy.101) | copy-start | bytes 6291460
  195.6 1.8 copy-start.18
  197.4 1.6 copy-start.5
  205.1 5.3 %copy-start.14 = (f32[128,8]{0,1:T(8,128)S(1)}, f32[128,8]{0,1:T(8,128)}, u32[]{:S(2)}) copy-start(f32[128,8]{0,1:T(8,128)} %param.28) | copy-start | bytes 12292
  205.1 82.9 %all-to-all-start.1 = ((bf16[32,2,24,2048]{3,2,1,0:T(8,128)(2,1)}), bf16[32,2,24,2048]{3,2,1,0:T(8,128)(2,1)}, u32[]{:S(2)}, u32[]{:S(2)}) async-start(bf16[32,2,24,2048]{3,2,1,0:T(8,128)(2,1)} %pad_maximum_fusion), calls=%async_computation.1 | async-start | bytes 12582912 | tf_op jit(solution)/shard_map/all_to_all | solution.py:188
  210.1 136.9 %all-reduce.6.cloned.1.call-start = ((), (), s32[]{:S(2)}) async-start(), calls=%async_computation.3 | async-start | bytes 1048576 | tf_op jit(solution)/shard_map/psum | solution.py:193
  307.8 8.9 %copy-start.16 = (f32[2,512]{1,0:T(2,128)S(1)}, f32[2,512]{1,0:T(2,128)}, u32[]{:S(2)}) copy-start(f32[2,512]{1,0:T(2,128)} %param.33) | copy-start | bytes 12292
  307.8 39.2 %copy-start.3 = (bf16[128,2048]{1,0:T(8,128)(2,1)S(1)}, bf16[128,2048]{1,0:T(8,128)(2,1)}, u32[]{:S(2)}) copy-start(bf16[128,2048]{1,0:T(8,128)(2,1)} %all-reduce.4.cloned.1.call-done) | copy-start | bytes 1572868
  307.8 40.6 %copy-start.11 = (f32[2048]{0:T(1024)S(1)}, f32[2048]{0:T(1024)}, u32[]{:S(2)}) copy-start(f32[2048]{0:T(1024)} %param.31) | copy-start | bytes 24580
  348.4 5.2 %copy-start.4 = (bf16[128,2048]{1,0:T(8,128)(2,1)}, bf16[128,2048]{1,0:T(8,128)(2,1)S(1)}, u32[]{:S(2)}) copy-start(bf16[128,2048]{1,0:T(8,128)(2,1)S(1)} %get-tuple-element.5) | copy-start | bytes 1572868
  363.9 1.9 copy-start.1
Sparse Core Ops, SparseCore 0:
  54.2 42.9 all-reduce.3
  307.9 39.0 all-reduce.5
where the time goes:
time: 374 us; the launch traced here: 373 us
  waiting for transfers between devices  213 us (57%)
  local copies, waits for them, and re-layouts  61.3 us (16%)
  other arithmetic  27.7 us (7%)
  matrix products  23.4 us (6%)
  blocking collectives  20.3 us (5%)
  between operations  14.6 us (4%)
  starting transfers between devices  12.9 us (3%)
    all_to_all x1, waiting for transfers between devices, per_device(): lax.all_to_all(produced, 'rep', split_axis=0, concat_axis=0, tiled=True)  77.5 us
    all_to_all x1, waiting for transfers between devices, per_device(): lax.all_to_all(outgoing, 'rep', split_axis=0, concat_axis=0, tiled=True)  69.3 us
    psum x1, waiting for transfers between devices, per_device(): lax.psum(attn_part.astype(jnp.bfloat16), 'tp').astype(jnp.float32)  35.4 us
    psum x1, waiting for transfers between devices, per_device(): lax.psum(partial_value.astype(jnp.bfloat16), 'tp').astype(jnp.float32)  30.3 us
    unnamed x48, local copies, waits for them, and re-layouts  24.7 us
    psum x2, blocking collectives, project_heads(): totals = lax.psum(squares, 'tp')  20.3 us
    gather x1, local copies, waits for them, and re-layouts, per_device(): returned.reshape(expert_count * full_cap, model_width)[flat_slot]  12.4 us
    dot_general x2, matrix products, project_heads(): jnp.dot(normed, weight.reshape(weight.shape[0], 3 * proj_width), preferre...  10.2 us
  transfers between devices with their start and end apart: 4, of which 4 were waited for; matrix products, arithmetic and copies ran while one was open for 7% of the time, Pallas kernels for 0%

commit v1 on v0

--- a/solution.py
+++ b/solution.py
@@ -190,7 +190,9 @@
     partial_value = jnp.sum(
         picked.reshape(row_count, choose_count, model_width) * expert_weights[:, :, None], axis=1
     )
-    moe_out = lax.psum(partial_value.astype(jnp.bfloat16), "tp").astype(jnp.float32)
+    moe_out = jnp.sum(lax.all_gather(partial_value.astype(jnp.bfloat16), "tp"), axis=0).astype(
+        jnp.float32
+    )
     hidden_out = (mid_stream.astype(jnp.float32) + moe_out).astype(jnp.bfloat16)
     next_input = rms_scale(hidden_out, next_gain)
     next_qkv_out = project_heads(next_input, next_qkv, next_norm_gains, position, HD)

time: 374 us -> 362 us (0.968)
  waiting for transfers between devices: 213 us -> 200 us
    psum x1 -> x0, waiting for transfers between devices: 30.3 us -> none  [per_device(): lax.psum(partial_value.astype(jnp.bfloat16), 'tp').astype(jnp.float32)]
    all_gather x0 -> x1, waiting for transfers between devices: none -> 18.1 us  [per_device(): lax.all_gather(partial_value.astype(jnp.bfloat16), 'tp')]
where the time goes in v1:
time: 362 us; the launch traced here: 361 us
  waiting for transfers between devices  200 us (55%)
  local copies, waits for them, and re-layouts  61.3 us (17%)
  other arithmetic  28.8 us (8%)
  matrix products  23.4 us (6%)
  blocking collectives  19.4 us (5%)
  between operations  14.6 us (4%)
  starting transfers between devices  12.9 us (4%)
    all_to_all x1, waiting for transfers between devices, per_device(): lax.all_to_all(produced, 'rep', split_axis=0, concat_axis=0, tiled=True)  77.5 us
    all_to_all x1, waiting for transfers between devices, per_device(): lax.all_to_all(outgoing, 'rep', split_axis=0, concat_axis=0, tiled=True)  69.3 us
    psum x1, waiting for transfers between devices, per_device(): lax.psum(attn_part.astype(jnp.bfloat16), 'tp').astype(jnp.float32)  35.4 us
    unnamed x48, local copies, waits for them, and re-layouts  24.8 us
    psum x2, blocking collectives, project_heads(): totals = lax.psum(squares, 'tp')  19.4 us
    all_gather x1, waiting for transfers between devices, per_device(): lax.all_gather(partial_value.astype(jnp.bfloat16), 'tp')  18.1 us
    gather x1, local copies, waits for them, and re-layouts, per_device(): returned.reshape(expert_count * full_cap, model_width)[flat_slot]  12.4 us
    dot_general x2, matrix products, project_heads(): jnp.dot(normed, weight.reshape(weight.shape[0], 3 * proj_width), preferre...  10.2 us
  transfers between devices with their start and end apart: 4, of which 4 were waited for; matrix products, arithmetic and copies ran while one was open for 7% of the time, Pallas kernels for 0%

profile of v1, /device:TPU:0, one launch (start us, length us, event | category | flops | bytes accessed | tf_op | source)
XLA Modules:
  0.0 360.7 jit_solution(18350566587746518104)
XLA Ops:
  7.2 9.0 %copy.73 = bf16[2048,3,512]{0,2,1:T(8,128)(2,1)} copy(bf16[2048,3,512]{2,0,1:T(8,128)(2,1)} %param.23) | data formatting | bytes 12582912 | tf_op args[6]
  16.4 5.0 %fusion.4 = f32[128,3,512]{2,0,1:T(8,128)S(1)} fusion(bf16[2048,3,512]{0,2,1:T(8,128)(2,1)} %copy.73, bf16[128,2048]{1,0:T(8,128)(2,1)S(1)} %copy-done.2, f32[2048]{0:T(1024)S(1)} %copy-done.9, f32[128]{0:T(128)S(1)} %add_rsqrt_fusion.4), kind=kOutput, calls=%fused_computation.9 | convolution fusion | flops 806354944 | bytes 7610880 | tf_op jit(solution)/shard_map/dot_general | solution.py:46
  22.4 10.8 %psum.21 = f32[128,2]{0,1:T(2,128)S(1)} all-reduce(f32[128,2]{0,1:T(2,128)S(1)} %fusion.33), channel_id=1, replica_groups=mesh['rep'=32,'tp'=4] {'tp'}, use_global_device_ids=true, to_apply=%region_6.7 | all-reduce | flops 256 | bytes 2048 | tf_op jit(solution)/shard_map/psum | solution.py:51
  41.6 2.4 copy.74
  44.1 2.3 pad_maximum_fusion.2
  46.4 3.7 %fusion.83 = (f32[4,128]{1,0:T(4,128)S(1)}, f32[4,128,1152]{2,1,0:T(8,128)}) fusion(bf16[1152,4,128]{0,2,1:T(8,128)(2,1)} %bitcast.131, pred[128,1152]{1,0:T(8,128)(4,1)S(1)} %pad_add_fusion, bf16[128,4,64]{2,0,1:T(8,128)(2,1)S(1)} %copy-done.7, bf16[128,4,64]{2,0,1:T(8,128)(2,1)S(1)} %get-tuple-element.18), kind=kOutput, calls=%fused_computation.156 | convolution fusion | flops 153617536 | bytes 3819520 | tf_op jit(solution)/shard_map/sub | solution.py:97
  50.1 2.6 fusion.10
  54.4 2.4 reduce-window.25
  57.5 4.3 %scatter_custom_fusion = s32[1536]{0:T(1024)S(1)} fusion(s32[1024]{0:T(1024)S(1)} %bitcast.139, s32[1024]{0:T(1024)S(1)} %add_select_fusion, s32[]{:T(128)} %constant.75.clone.1), kind=kCustom, calls=%fused_computation.120 | custom fusion | bytes 6148 | tf_op jit(solution)/shard_map/scatter | solution.py:181
  61.8 35.4 %all-reduce.3.cloned.1.call-done = bf16[128,2048]{1,0:T(8,128)(2,1)} async-done(((bf16[128,2048]{1,0:T(8,128)(2,1)}), bf16[128,2048]{1,0:T(8,128)(2,1)}) %all-reduce.3.cloned.1.call-update) | async-done | bytes 524304 | tf_op jit(solution)/shard_map/psum | solution.py:168
  99.8 7.1 %gather_fusion = bf16[1536,2048]{1,0:T(8,128)(2,1)} fusion(bf16[129,2048]{1,0:T(8,128)(2,1)S(1)} %concatenate.33, s32[2048]{0:T(1024)S(1)} %pad_clamp_fusion), kind=kCustom, calls=%fused_computation | custom fusion | bytes 12589056 | tf_op jit(solution)/shard_map/gather | solution.py:184
  106.9 7.5 %all-to-all-start = ((bf16[32,2,24,2048]{3,2,1,0:T(8,128)(2,1)}), bf16[32,2,24,2048]{3,2,1,0:T(8,128)(2,1)}, u32[]{:S(2)}, u32[]{:S(2)}) async-start(bf16[32,2,24,2048]{3,2,1,0:T(8,128)(2,1)} %bitcast.120), calls=%async_computation | async-start | bytes 12582912 | tf_op jit(solution)/shard_map/all_to_all | solution.py:186
  114.5 4.7 %fusion.78 = (bf16[1,2048,2,256]{3,2,1,0:T(2,128)(2,1)S(1)}, bf16[1,2048,2,256]{3,2,1,0:T(2,128)(2,1)S(1)}) fusion(bf16[2,2048,2,256]{3,2,1,0:T(2,128)(2,1)} %param.29), kind=kLoop, calls=%fused_computation.151 | loop fusion | bytes 8388608 | tf_op jit(solution)/shard_map/slice | solution.py:119
  122.8 69.3 %all-to-all-done = bf16[32,2,24,2048]{3,2,1,0:T(8,128)(2,1)} async-done(((bf16[32,2,24,2048]{3,2,1,0:T(8,128)(2,1)}), bf16[32,2,24,2048]{3,2,1,0:T(8,128)(2,1)}, u32[]{:S(2)}, u32[]{:S(2)}) %all-to-all-start) | async-done | bytes 6291488 | tf_op jit(solution)/shard_map/all_to_all | solution.py:186
  192.2 3.4 fusion.77
  201.8 3.2 pad_maximum_fusion
  205.1 5.0 %all-to-all-start.1 = ((bf16[32,2,24,2048]{3,2,1,0:T(8,128)(2,1)}), bf16[32,2,24,2048]{3,2,1,0:T(8,128)(2,1)}, u32[]{:S(2)}, u32[]{:S(2)}) async-start(bf16[32,2,24,2048]{3,2,1,0:T(8,128)(2,1)} %pad_maximum_fusion), calls=%async_computation.1 | async-start | bytes 12582912 | tf_op jit(solution)/shard_map/all_to_all | solution.py:188
  210.5 77.5 %all-to-all-done.1 = bf16[32,2,24,2048]{3,2,1,0:T(8,128)(2,1)} async-done(((bf16[32,2,24,2048]{3,2,1,0:T(8,128)(2,1)}), bf16[32,2,24,2048]{3,2,1,0:T(8,128)(2,1)}, u32[]{:S(2)}, u32[]{:S(2)}) %all-to-all-start.1) | async-done | bytes 6291488 | tf_op jit(solution)/shard_map/all_to_all | solution.py:188
  288.0 12.4 %gather_fusion.1 = bf16[1024,2048]{1,0:T(8,128)(2,1)} fusion(bf16[1536,2048]{1,0:T(8,128)(2,1)} %bitcast.33, s32[1024]{0:T(1024)S(1)} %broadcast_clamp_fusion), kind=kCustom, calls=%fused_computation.1 | custom fusion | bytes 8392704 | tf_op jit(solution)/shard_map/gather | solution.py:189
  300.4 7.3 %fusion.1 = bf16[128,2048]{1,0:T(8,128)(2,1)} fusion(bf16[1024,2048]{1,0:T(8,128)(2,1)} %gather_fusion.1, f32[128,8]{1,0:T(8,128)S(1)} %copy.88), kind=kLoop, calls=%fused_computation.5 | loop fusion | flops 6029312 | bytes 4722688 | tf_op jit(solution)/shard_map/reduce_sum | solution.py:190
  307.8 8.9 %copy.89 = bf16[2048,3,512]{0,2,1:T(8,128)(2,1)} copy(bf16[2048,3,512]{2,0,1:T(8,128)(2,1)} %param.32) | data formatting | bytes 12582912 | tf_op args[15]
  316.7 18.1 %all-gather.3.cloned.1.call-done = bf16[512,2048]{1,0:T(8,128)(2,1)} async-done(((bf16[128,2048]{1,0:T(8,128)(2,1)}), bf16[512,2048]{1,0:T(8,128)(2,1)}) %all-gather.3.cloned.1.call-update) | async-done | bytes 2097168 | tf_op jit(solution)/shard_map/all_gather | solution.py:193
  337.3 5.2 %fusion.2 = f32[128,3,512]{2,0,1:T(8,128)S(1)} fusion(bf16[2048,3,512]{0,2,1:T(8,128)(2,1)} %copy.89, bf16[128,2048]{1,0:T(8,128)(2,1)S(1)} %get-tuple-element.5, f32[2048]{0:T(1024)S(1)} %copy-done.11, f32[128]{0:T(128)S(1)} %add_rsqrt_fusion.2), kind=kOutput, calls=%fused_computation.7 | convolution fusion | flops 806354944 | bytes 7610880 | tf_op jit(solution)/shard_map/dot_general | solution.py:46
  343.0 8.6 %psum.23 = f32[128,2]{0,1:T(2,128)S(1)} all-reduce(f32[128,2]{0,1:T(2,128)S(1)} %fusion.32), channel_id=1, replica_groups=mesh['rep'=32,'tp'=4] {'tp'}, use_global_device_ids=true, to_apply=%region_21.22 | all-reduce | flops 256 | bytes 2048 | tf_op jit(solution)/shard_map/psum | solution.py:51
  (126 shorter events, 29.7 us)
Async XLA Ops:
  7.2 45.6 %copy-start = (bf16[512,2048]{1,0:T(8,128)(2,1)S(1)}, bf16[512,2048]{1,0:T(8,128)(2,1)}, u32[]{:S(2)}) copy-start(bf16[512,2048]{1,0:T(8,128)(2,1)} %param.25) | copy-start | bytes 6291460
  7.2 9.1 %copy-start.2 = (bf16[128,2048]{1,0:T(8,128)(2,1)S(1)}, bf16[128,2048]{1,0:T(8,128)(2,1)}, u32[]{:S(2)}) copy-start(bf16[128,2048]{1,0:T(8,128)(2,1)} %param.17) | copy-start | bytes 1572868
  7.2 9.3 %copy-start.9 = (f32[2048]{0:T(1024)S(1)}, f32[2048]{0:T(1024)}, u32[]{:S(2)}) copy-start(f32[2048]{0:T(1024)} %param.22) | copy-start | bytes 24580
  7.2 90.0 %all-reduce.3.cloned.1.call-start = ((), (), s32[]{:S(2)}) async-start(), calls=%async_computation.2 | async-start | bytes 1048576 | tf_op jit(solution)/shard_map/psum | solution.py:168
  21.5 11.8 %copy-start.15 = (f32[2,512]{1,0:T(2,128)S(1)}, f32[2,512]{1,0:T(2,128)}, u32[]{:S(2)}) copy-start(f32[2,512]{1,0:T(2,128)} %param.24) | copy-start | bytes 12292
  21.5 11.8 %copy-start.19 = (s32[1,4]{1,0:T(1,128)S(1)}, s32[1,4]{1,0:T(1,128)}, u32[]{:S(2)}) copy-start(s32[1,4]{1,0:T(1,128)} %param.18) | copy-start | bytes 52
  33.5 1.9 copy-start.12
  35.5 3.4 copy-start.17
  35.5 3.7 %copy-start.13 = (s32[128]{0:T(128)S(1)}, s32[128]{0:T(128)}, u32[]{:S(2)}) copy-start(s32[128]{0:T(128)} %copy-done.12) | copy-start | bytes 1540
  41.6 4.7 %copy-start.7 = (bf16[128,4,64]{2,0,1:T(8,128)(2,1)S(1)}, bf16[128,4,64]{2,0,1:T(8,128)(2,1)}, u32[]{:S(2)}) copy-start(bf16[128,4,64]{2,0,1:T(8,128)(2,1)} %get-tuple-element.19) | copy-start | bytes 196612
  52.7 1.3 copy-start.8
  54.0 44.5 %copy-start.10 = (f32[2048]{0:T(1024)S(1)}, f32[2048]{0:T(1024)}, u32[]{:S(2)}) copy-start(f32[2048]{0:T(1024)} %param.26) | copy-start | bytes 24580
  106.9 85.2 %all-to-all-start = ((bf16[32,2,24,2048]{3,2,1,0:T(8,128)(2,1)}), bf16[32,2,24,2048]{3,2,1,0:T(8,128)(2,1)}, u32[]{:S(2)}, u32[]{:S(2)}) async-start(bf16[32,2,24,2048]{3,2,1,0:T(8,128)(2,1)} %bitcast.120), calls=%async_computation | async-start | bytes 12582912 | tf_op jit(solution)/shard_map/all_to_all | solution.py:186
  122.8 72.8 %copy-start.6 = (bf16[256,8,2,256]{3,1,2,0:T(8,128)(2,1)S(1)}, bf16[256,8,2,256]{3,1,2,0:T(8,128)(2,1)}, u32[]{:S(2)}) copy-start(bf16[256,8,2,256]{3,1,2,0:T(8,128)(2,1)} %copy.101) | copy-start | bytes 6291460
  195.6 1.8 copy-start.18
  197.4 1.6 copy-start.5
  205.1 5.3 %copy-start.14 = (f32[128,8]{0,1:T(8,128)S(1)}, f32[128,8]{0,1:T(8,128)}, u32[]{:S(2)}) copy-start(f32[128,8]{0,1:T(8,128)} %param.28) | copy-start | bytes 12292
  205.1 82.9 %all-to-all-start.1 = ((bf16[32,2,24,2048]{3,2,1,0:T(8,128)(2,1)}), bf16[32,2,24,2048]{3,2,1,0:T(8,128)(2,1)}, u32[]{:S(2)}, u32[]{:S(2)}) async-start(bf16[32,2,24,2048]{3,2,1,0:T(8,128)(2,1)} %pad_maximum_fusion), calls=%async_computation.1 | async-start | bytes 12582912 | tf_op jit(solution)/shard_map/all_to_all | solution.py:188
  210.1 124.8 %all-gather.3.cloned.1.call-start = ((), (), s32[]{:S(2)}) async-start(), calls=%async_computation.3 | async-start | bytes 2621440 | tf_op jit(solution)/shard_map/all_gather | solution.py:193
  307.8 9.0 %copy-start.16 = (f32[2,512]{1,0:T(2,128)S(1)}, f32[2,512]{1,0:T(2,128)}, u32[]{:S(2)}) copy-start(f32[2,512]{1,0:T(2,128)} %param.33) | copy-start | bytes 12292
  316.7 20.2 %copy-start.3 = (bf16[128,2048]{1,0:T(8,128)(2,1)S(1)}, bf16[128,2048]{1,0:T(8,128)(2,1)}, u32[]{:S(2)}) copy-start(bf16[128,2048]{1,0:T(8,128)(2,1)} %all-reduce.3.cloned.1.call-done) | copy-start | bytes 1572868
  334.9 2.5 copy-start.11
  337.3 5.2 %copy-start.4 = (bf16[128,2048]{1,0:T(8,128)(2,1)}, bf16[128,2048]{1,0:T(8,128)(2,1)S(1)}, u32[]{:S(2)}) copy-start(bf16[128,2048]{1,0:T(8,128)(2,1)S(1)} %get-tuple-element.5) | copy-start | bytes 1572868
  351.9 1.9 copy-start.1
Sparse Core Ops, SparseCore 0:
  54.2 42.9 all-reduce.2
  307.9 26.9 all-gather.2
